TPU v7x, 256 devices: a whole 4x4x8 slice. The times are simulated.
256 devices in a mesh: sub: 8 (over x, core), tm: 32 (over z, y).
Axes of the slice: x: 4, y: 4, z: 8, core: 2. Of those that a mesh axis runs over, the one named last changes fastest.
Arguments:
- spectra: bfloat16 [2048, 131072], P('sub', 'tm'), may hold values from -2000 to 2000
- chan_mask: int32 [2048], P('sub'), may hold values from 0 to 1
- delay_step: int32 [2048], replicated, may hold values from 2 to 18, as said below
Outputs:
- peaks: float32 [512, 8, 512], P('sub', None, 'tm')
Inputs may be any that keep to these rules, and one draw needn't show every extreme that they name: `delay_step`: non-decreasing in frequency order; the first entry is 2 and the last 18.
All inputs are finite; a program needn't handle non-finite values.
Results may differ from a plain program's by a relative error of at most 0.0003.
Values may be sent and summed in bfloat16 or wider, within the bound.
A program may use at most 64 MiB of HBM per device.

v0:
```python
import math

import jax
import jax.numpy as jnp
from jax import lax
from jax.sharding import PartitionSpec as P

WIDTHS = 8
BLOCK = 256


def shortened(shard):

    def short(part):
        return part.astype(jnp.bfloat16) if part.dtype == jnp.float32 else part

    return jax.tree.map(short, shard)


def shifted(block, axis, distance):
    devices = range(lax.axis_size(axis))
    route = [(i - distance, i) for i in devices if i - distance in devices]
    return lax.ppermute(block, axis, route)


def from_partner(block, axis, bit):
    count = lax.axis_size(axis)
    route = []
    for low in range(count):
        high = low | 1 << bit
        if high != low and high < count:
            route += [(low, high), (high, low)]
    return lax.ppermute(block, axis, route)


def reverse_bits(number, bit_count):
    result = jnp.zeros((), jnp.int32)
    for bit_place in range(bit_count):
        result = result + ((number >> bit_place & 1) << bit_count - 1 - bit_place)
    return result


def split_shifts(prefix, starts, half_span, trial_ids):
    early_span = prefix[starts + half_span] - prefix[starts]
    later_span = prefix[starts + 2 * half_span] - prefix[starts + half_span]
    return trial_ids[None, :] * early_span[:, None] // (early_span + later_span)[:, None]


def slide_rows(row_block, amounts, length):

    def single(one_row, amount):
        return lax.dynamic_slice_in_dim(one_row, amount, length)

    return jax.vmap(jax.vmap(single, (None, 0)), (0, 0))(row_block, amounts)


def fetch_tail(row_block, length):
    tail_rows = shifted(shortened(row_block[:, :length]), "tm", -1)
    return jnp.concatenate([row_block, tail_rows], axis=1)


def local(spectra, chan_mask, delay_step):
    sub_count = lax.axis_size("sub")
    time_count = lax.axis_size("tm")
    cross_levels = sub_count.bit_length() - 1
    sub_index = lax.axis_index("sub")
    channels, samples = spectra.shape
    rows_dev = channels // 4
    half_rows = rows_dev // 2
    local_levels = channels.bit_length() - 1
    total_time = samples * time_count
    widest = 2 ** (WIDTHS - 1)
    as_float = spectra.astype(jnp.float32)
    totals = lax.psum((jnp.sum(as_float, axis=1), jnp.sum(as_float * as_float, axis=1)), "tm")
    centre = totals[0] / total_time
    spread = lax.rsqrt(totals[1] / total_time - centre * centre + 1e-05)
    weight = chan_mask.astype(jnp.float32)
    normed = (spectra.astype(jnp.float32) - centre[:, None]) * spread[:, None] * weight[:, None]
    columns = normed.shape[1]
    planes = jnp.sum(normed.reshape(rows_dev, 4, columns), axis=1)[:, None, :]
    position = reverse_bits(sub_index, cross_levels)
    prefix = jnp.concatenate([jnp.zeros((1,), jnp.int32), jnp.cumsum(delay_step)])
    for merge_level in range(3, local_levels + 1):
        band_count = channels >> merge_level
        row_depth = 2 ** (merge_level - 3)
        paired = planes.reshape(band_count, 2, row_depth, columns)
        lower_rows = paired[:, 0].reshape(band_count * row_depth, columns)
        upper_rows = paired[:, 1].reshape(band_count * row_depth, columns)
        upper_rows = fetch_tail(upper_rows, row_depth)
        starts = position * channels + jnp.arange(band_count, dtype=jnp.int32) * 2**merge_level
        trial_ids = jnp.arange(2 * row_depth, dtype=jnp.int32)
        shifts = split_shifts(prefix, starts, 2 ** (merge_level - 1), trial_ids)
        moved = slide_rows(upper_rows, shifts.reshape(band_count * row_depth, 2), columns)
        planes = (lower_rows[:, None, :] + moved).reshape(band_count, 2 * row_depth, columns)
    plane_rows = planes.reshape(rows_dev, columns)
    for merge_step in range(1, cross_levels + 1):
        pair_bit = cross_levels - merge_step
        half_side = sub_index >> pair_bit & 1
        row_depth = rows_dev * 2 ** (merge_step - 1)
        plane_rows = fetch_tail(plane_rows, row_depth)
        kept_rows = lax.dynamic_slice_in_dim(plane_rows, half_side * half_rows, half_rows, 0)
        sent_rows = lax.dynamic_slice_in_dim(plane_rows, (1 - half_side) * half_rows, half_rows, 0)
        partner = from_partner(sent_rows, "sub", pair_bit)
        lower_rows = jnp.where(half_side == 0, kept_rows, partner)[:, :columns]
        upper_rows = jnp.where(half_side == 0, partner, kept_rows)
        half_span = 2 ** (merge_step - 1) * channels
        band_start = (position >> merge_step << merge_step) * channels
        trial_ids = (sub_index >> pair_bit) * rows_dev + jnp.arange(rows_dev, dtype=jnp.int32)
        shifts = split_shifts(prefix, band_start[None], half_span, trial_ids)
        moved = slide_rows(upper_rows, shifts.reshape(half_rows, 2), columns)
        plane_rows = (lower_rows[:, None, :] + moved).reshape(rows_dev, columns)
    power_sum = lax.psum(jnp.sum(plane_rows * plane_rows, axis=1), "tm")
    level_rms = jnp.sqrt(power_sum / total_time + 1e-06)
    scaled = plane_rows / level_rms[:, None]
    prior_rows = shifted(scaled[:, samples - widest + 1 :], "tm", 1)
    running = jnp.concatenate([prior_rows, scaled], axis=1)
    maxima = []
    for section in range(WIDTHS):
        box_width = 2**section
        if section > 0:
            running = running[:, box_width // 2 :] + running[:, : -(box_width // 2)]
        snr_rows = running[:, -samples:] / math.sqrt(box_width)
        maxima.append(jnp.max(snr_rows.reshape(rows_dev, samples // BLOCK, BLOCK), axis=2))
    return jnp.stack(maxima, axis=1)


def solution(mesh):
    in_specs = (P("sub", "tm"), P("sub"), P())
    out_specs = P("sub", None, "tm")
    return jax.shard_map(local, mesh=mesh, in_specs=in_specs, out_specs=out_specs, check_vma=False)
```

profile of v0, /device:TPU:128, one launch (start us, length us, event | category | flops | bytes accessed | tf_op | source)
XLA Modules:
  0.0 1922.0 jit_solution(16558146293047687703)
XLA Ops:
  0.8 2.4 convert_reduce_fusion
  3.3 72.2 %all-reduce = (f32[256]{0:T(256)S(1)}, f32[256]{0:T(256)S(1)}) all-reduce(f32[256]{0:T(256)S(1)} %get-tuple-element.211, f32[256]{0:T(256)S(1)} %get-tuple-element.210), channel_id=1, replica_groups=mesh['sub'=8,'tm'=32] {'tm'}, use_global_device_ids=true, to_apply=%region_3.0 | all-reduce | flops 512 | bytes 4096 | tf_op jit(solution)/shard_map/psum | solution.py:74
  75.5 2.9 fusion.1
  78.4 5.2 reshape.1330
  83.5 4.8 reduce_sum.40
  126.3 149.4 %while.21 = (s32[]{:T(128)}, f32[32,4097]{1,0:T(8,128)S(1)}, s32[64,2]{0,1:T(2,128)S(1)}, f32[64,4096]{1,0:T(8,128)S(1)}, s32[]{:T(128)}, /*index=5*/s32[]{:T(128)}) while((s32[]{:T(128)}, f32[32,4097]{1,0:T(8,128)S(1)}, s32[64,2]{0,1:T(2,128)S(1)}, f32[64,4096]{1,0:T(8,128)S(1)}, s32[]{:T(128)}, /*index=5*/s32[]{:T(128)}) %tuple.247), condition=%wide.while_cond, body=%wide.while_body.sunk | while | flops 2 | bytes 65657 | solution.py:52
  280.5 2.5 collective-permute-done.1
  283.1 152.7 %while.22 = (s32[]{:T(128)}, f32[32,4098]{1,0:T(8,128)S(1)}, s32[64,2]{0,1:T(2,128)S(1)}, f32[64,4096]{1,0:T(8,128)S(1)}, s32[]{:T(128)}, /*index=5*/s32[]{:T(128)}) while((s32[]{:T(128)}, f32[32,4098]{1,0:T(8,128)S(1)}, s32[64,2]{0,1:T(2,128)S(1)}, f32[64,4096]{1,0:T(8,128)S(1)}, s32[]{:T(128)}, /*index=5*/s32[]{:T(128)}) %tuple.250), condition=%wide.while_cond.1, body=%wide.while_body.1.sunk | while | flops 2 | bytes 65657 | solution.py:52
  439.6 5.5 collective-permute-start.2
  446.4 157.4 %while.23 = (s32[]{:T(128)}, f32[32,4100]{1,0:T(8,128)S(1)}, s32[64,2]{0,1:T(2,128)S(1)}, f32[64,4096]{1,0:T(8,128)S(1)}, s32[]{:T(128)}, /*index=5*/s32[]{:T(128)}) while((s32[]{:T(128)}, f32[32,4100]{1,0:T(8,128)S(1)}, s32[64,2]{0,1:T(2,128)S(1)}, f32[64,4096]{1,0:T(8,128)S(1)}, s32[]{:T(128)}, /*index=5*/s32[]{:T(128)}) %tuple.253), condition=%wide.while_cond.2, body=%wide.while_body.2.sunk | while | flops 2 | bytes 65657 | solution.py:52
  607.9 7.4 collective-permute-start.3
  616.8 157.4 %while.24 = (s32[]{:T(128)}, f32[32,4104]{1,0:T(8,128)S(1)}, s32[64,2]{0,1:T(2,128)S(1)}, f32[64,4096]{1,0:T(8,128)S(1)}, s32[]{:T(128)}, /*index=5*/s32[]{:T(128)}) while((s32[]{:T(128)}, f32[32,4104]{1,0:T(8,128)S(1)}, s32[64,2]{0,1:T(2,128)S(1)}, f32[64,4096]{1,0:T(8,128)S(1)}, s32[]{:T(128)}, /*index=5*/s32[]{:T(128)}) %tuple.256), condition=%wide.while_cond.3, body=%wide.while_body.3.sunk | while | flops 2 | bytes 65657 | solution.py:52
  778.3 7.5 collective-permute-start.4
  787.3 157.4 %while.25 = (s32[]{:T(128)}, f32[32,4112]{1,0:T(8,128)S(1)}, s32[64,2]{0,1:T(2,128)S(1)}, f32[64,4096]{1,0:T(8,128)S(1)}, s32[]{:T(128)}, /*index=5*/s32[]{:T(128)}) while((s32[]{:T(128)}, f32[32,4112]{1,0:T(8,128)S(1)}, s32[64,2]{0,1:T(2,128)S(1)}, f32[64,4096]{1,0:T(8,128)S(1)}, s32[]{:T(128)}, /*index=5*/s32[]{:T(128)}) %tuple.259), condition=%wide.while_cond.4, body=%wide.while_body.4.sunk | while | flops 2 | bytes 65657 | solution.py:52
  948.8 7.5 collective-permute-start.5
  957.8 157.4 %while.26 = (s32[]{:T(128)}, f32[32,4128]{1,0:T(8,128)S(1)}, s32[64,2]{0,1:T(2,128)S(1)}, f32[64,4096]{1,0:T(8,128)S(1)}, s32[]{:T(128)}, /*index=5*/s32[]{:T(128)}) while((s32[]{:T(128)}, f32[32,4128]{1,0:T(8,128)S(1)}, s32[64,2]{0,1:T(2,128)S(1)}, f32[64,4096]{1,0:T(8,128)S(1)}, s32[]{:T(128)}, /*index=5*/s32[]{:T(128)}) %tuple.262), condition=%wide.while_cond.8, body=%wide.while_body.8.sunk | while | flops 2 | bytes 65657 | solution.py:52
  1118.4 7.5 collective-permute-start.6
  1127.4 3.5 collective-permute-start.7
  1131.1 7.6 collective-permute-done.7
  1139.7 210.4 %while.27 = (s32[]{:T(128)}, f32[32,4160]{1,0:T(8,128)}, s32[64,2]{0,1:T(2,128)S(1)}, f32[64,4096]{1,0:T(8,128)S(1)}, s32[]{:T(128)}, /*index=5*/s32[]{:T(128)}) while((s32[]{:T(128)}, f32[32,4160]{1,0:T(8,128)}, s32[64,2]{0,1:T(2,128)S(1)}, f32[64,4096]{1,0:T(8,128)S(1)}, s32[]{:T(128)}, /*index=5*/s32[]{:T(128)}) %tuple.265), condition=%wide.while_cond.12, body=%wide.while_body.12.sunk | while | flops 2 | bytes 65657 | solution.py:52
  1352.4 7.5 collective-permute-start.8
  1363.2 7.7 collective-permute-done.9
  1371.8 210.4 %while.28 = (s32[]{:T(128)}, f32[32,4224]{1,0:T(8,128)}, s32[64,2]{0,1:T(2,128)S(1)}, f32[64,4096]{1,0:T(8,128)S(1)}, s32[]{:T(128)}, /*index=5*/s32[]{:T(128)}) while((s32[]{:T(128)}, f32[32,4224]{1,0:T(8,128)}, s32[64,2]{0,1:T(2,128)S(1)}, f32[64,4096]{1,0:T(8,128)S(1)}, s32[]{:T(128)}, /*index=5*/s32[]{:T(128)}) %tuple.268), condition=%wide.while_cond.16, body=%wide.while_body.16.sunk | while | flops 2 | bytes 65657 | solution.py:52
  1584.5 7.5 collective-permute-start.10
  1596.6 213.4 %while.29 = (s32[]{:T(128)}, f32[32,4352]{1,0:T(8,128)}, s32[64,2]{0,1:T(2,128)S(1)}, f32[64,4096]{1,0:T(8,128)S(1)}, s32[]{:T(128)}, /*index=5*/s32[]{:T(128)}) while((s32[]{:T(128)}, f32[32,4352]{1,0:T(8,128)}, s32[64,2]{0,1:T(2,128)S(1)}, f32[64,4096]{1,0:T(8,128)S(1)}, s32[]{:T(128)}, /*index=5*/s32[]{:T(128)}) %tuple.271), condition=%wide.while_cond.20, body=%wide.while_body.20.sunk | while | flops 2 | bytes 65657 | solution.py:52
  1600.6 2.2 dynamic-slice.155
  1604.0 2.2 dynamic-slice.155
  1607.3 2.2 dynamic-slice.155
  1610.7 2.2 dynamic-slice.155
  1617.3 2.2 dynamic-slice.155
  1620.7 2.2 dynamic-slice.155
  1624.0 2.2 dynamic-slice.155
  1627.3 2.2 dynamic-slice.155
  1634.0 2.2 dynamic-slice.155
  1637.3 2.2 dynamic-slice.155
  1640.7 2.2 dynamic-slice.155
  1647.3 2.2 dynamic-slice.155
  1650.7 2.2 dynamic-slice.155
  1654.0 2.2 dynamic-slice.155
  1657.3 2.2 dynamic-slice.155
  1664.0 2.2 dynamic-slice.155
  1667.3 2.2 dynamic-slice.155
  1670.7 2.2 dynamic-slice.155
  1674.0 2.2 dynamic-slice.155
  1813.5 75.3 %psum.23 = f32[64]{0:T(128)S(1)} all-reduce(f32[64]{0:T(128)S(1)} %reduce_sum.42), channel_id=1, replica_groups=mesh['sub'=8,'tm'=32] {'tm'}, use_global_device_ids=true, to_apply=%region_8.10 | all-reduce | flops 64 | bytes 512 | tf_op jit(solution)/shard_map/psum | solution.py:112
  1891.5 7.0 collective-permute-done.12
  1907.4 2.5 copy.108
  1911.5 2.6 copy.109
  (2568 shorter events, 1598.4 us)
Async XLA Ops:
  0.0 75.5 %copy-start = (bf16[256,4096]{1,0:T(8,128)(2,1)S(1)}, bf16[256,4096]{1,0:T(8,128)(2,1)}, u32[]{:S(2)}) copy-start(bf16[256,4096]{1,0:T(8,128)(2,1)} %param.5) | copy-start | bytes 6291460
  90.9 2.5 copy-start.1
  91.3 34.9 %collective-permute-start = (bf16[32,1]{1,0:T(8,128)(2,1)S(1)}, bf16[32,1]{1,0:T(8,128)(2,1)S(1)}, u32[]{:S(2)}, u32[]{:S(2)}) collective-permute-start(bf16[32,1]{1,0:T(8,128)(2,1)S(1)} %slice.475), channel_id=1, source_target_pairs={{1,0},{2,1},{3,2},{4,3},{5,4},{6,5},{7,6},{8,7},{9,8},{10,9},{11,1... | collective-permute-start | bytes 200 | tf_op jit(solution)/shard_map/ppermute | solution.py:23
  277.4 5.5 collective-permute-start.1
  439.6 6.7 collective-permute-start.2
  607.9 8.7 collective-permute-start.3
  778.3 8.9 collective-permute-start.4
  948.8 8.9 collective-permute-start.5
  1118.4 8.9 collective-permute-start.6
  1127.4 11.4 collective-permute-start.7
  1352.4 9.0 collective-permute-start.8
  1361.4 9.4 collective-permute-start.9
  1584.5 9.1 collective-permute-start.10
  1593.7 2.0 collective-permute-start.11
  1889.4 9.1 collective-permute-start.12
  1920.6 0.6 copy-start.2
where the time goes:
time: 1940 us; the launch traced here: 1920 us
  local copies, waits for them, and re-layouts  1600 us (82%)
  blocking collectives  147 us (8%)
  starting transfers between devices  61.7 us (3%)
  other arithmetic  41.9 us (2%)
  waiting for transfers between devices  34.3 us (2%)
    gather x2304, local copies, waits for them, and re-layouts  1550 us
    psum x1, blocking collectives, local(): power_sum = lax.psum(jnp.sum(plane_rows * plane_rows, axis=1), 'tm')  75.3 us
    psum x1, blocking collectives, local(): lax.psum((jnp.sum(as_float, axis=1), jnp.sum(as_float * as_float, axis=1)...  72.2 us
    ppermute x10, starting transfers between devices, shifted(): return lax.ppermute(block, axis, route)  56.5 us
  transfers between devices with their start and end apart: 13, of which 11 were waited for; matrix products, arithmetic and copies ran while one was open for 1% of the time, Pallas kernels for 0%

commit v1 on v0

v1 whole, which is shorter than its diff:
```python
import functools
import math

import jax
import jax.numpy as jnp
from jax import lax
from jax.experimental import pallas as pl
from jax.experimental.pallas import tpu as pltpu
from jax.sharding import PartitionSpec as P

MESH = pl.DeviceIdType.MESH
F32 = jnp.float32
BF16 = jnp.bfloat16
I32 = jnp.int32

WIDTHS = 8
LANES = 128
LEFT = 1
RIGHT = 4
SPAN = 40


def reversed_bits(number, bit_count):
    result = 0
    for place in range(bit_count):
        result = result + ((number >> place) % 2) * 2 ** (bit_count - 1 - place)
    return result


def iota(shape, dim):
    return lax.broadcasted_iota(I32, shape, dim)


def remote(src, dst, send_sem, recv_sem, device_id):
    return pltpu.make_async_remote_copy(
        src_ref=src,
        dst_ref=dst,
        send_sem=send_sem,
        recv_sem=recv_sem,
        device_id=device_id,
        device_id_type=MESH,
    )


def delay_table(geo, position, sub_index, delay_ref):
    rows = geo.rows
    level_rows = []
    local = delay_ref[pl.ds(2 * position, 2), :].astype(F32)
    local = jnp.concatenate([local[0:1], local[1:2]], axis=1)
    local = jnp.broadcast_to(local, (8, geo.channels)).astype(BF16)
    channel = iota((rows, geo.channels), 1)
    row = iota((rows, geo.channels), 0)
    blocks = jnp.sum(delay_ref[...].astype(F32), axis=1, keepdims=True)
    block = iota((2 * geo.n_sub, rows), 0) // 2
    lane_row = iota((1, rows), 1)
    for level in range(4, geo.local_levels + geo.cross_levels + 1):
        if level <= geo.local_levels:
            depth = level - 2
            band = row >> depth
            spans = []
            for mask in ((channel >> (level - 1)) == 2 * band, (channel >> level) == band):
                spans.append(
                    lax.dot_general(
                        local, mask.astype(F32).astype(BF16), (((1,), (1,)), ((), ())), preferred_element_type=F32
                    )[0:1]
                )
            trial = lane_row & (2**depth - 1)
        else:
            depth = level - 2 - geo.cross_levels
            band = iota((2 * geo.n_sub, rows), 1) >> depth
            up = level - geo.local_levels
            spans = []
            for mask in ((block >> (up - 1)) == 2 * band, (block >> up) == band):
                spans.append(jnp.sum(jnp.where(mask, blocks, 0.0), axis=0, keepdims=True))
            trial = sub_index * 2**depth + (lane_row & (2**depth - 1))
        early = spans[0].astype(I32)
        whole = jnp.maximum(spans[1].astype(I32), 1)
        product = trial * early
        shift = (product.astype(F32) / whole.astype(F32)).astype(I32)
        rest = product - shift * whole
        shift = shift + jnp.where(rest >= whole, 1, 0) - jnp.where(rest < 0, 1, 0)
        level_rows.append(jnp.clip(shift, 0, 2 ** (level - 3) - 1))
    table = jnp.concatenate(level_rows, axis=0)
    return jnp.concatenate([table, table], axis=1)


def merge(geo, src, dst, table, level, fan, wide=False):
    lane = iota((SPAN, LANES), 1)
    step = geo.tiles

    def pair(p, carry):
        low = p + (p // fan) * fan
        base = low * step
        upper = base + fan * step
        lower_rows = src[pl.ds(base, SPAN), :]
        if not wide:
            here = src[pl.ds(upper, SPAN), :]
            after = src[pl.ds(upper + 1, SPAN), :]
        for i in range(2):
            shift = table[level - 4, 2 * p + i]
            if wide:
                start = upper + (shift >> 7)
                shift = shift & (LANES - 1)
                here = src[pl.ds(start, SPAN), :]
                after = src[pl.ds(start + 1, SPAN), :]
            mixed = jnp.where(lane >= shift, here, after)
            moved = pltpu.roll(mixed, (LANES - shift) & (LANES - 1), 1)
            dst[pl.ds((2 * p + i) * step, SPAN), :] = lower_rows + moved
        return carry

    lax.fori_loop(0, geo.rows // 2, pair, 0, unroll=2)


def first_merge(geo, src, dst, table):
    lane = iota((SPAN, LANES), 1)
    step = geo.tiles

    def band(s, carry):
        base = 2 * s * step
        lower_rows = src[pl.ds(base, SPAN), :]
        here = src[pl.ds(base + step, SPAN), :]
        after = src[pl.ds(base + step + 1, SPAN), :]
        for i in range(4):
            shift = table[0, 4 * s + i]
            mixed = jnp.where(lane >= shift, here, after)
            moved = pltpu.roll(mixed, (LANES - shift) & (LANES - 1), 1)
            dst[pl.ds((4 * s + i) * step, SPAN), :] = lower_rows + moved
        return carry

    lax.fori_loop(0, geo.rows // 4, band, 0)


class Ring:
    def __init__(self, slots, me, count, device, send, recv):
        self.slots, self.me, self.count, self.device = slots, me, count, device
        self.send, self.recv = send, recv

    def copy(self, k, slot):
        peer = lax.rem(self.me + k, self.count)
        return remote(
            self.slots.at[self.me], self.slots.at[slot], self.send.at[k], self.recv.at[slot], self.device(peer)
        )

    def start(self, value):
        self.slots[pl.ds(self.me, 1)] = value[None]
        for k in range(1, self.count):
            self.copy(k, self.me).start()

    def total(self):
        for k in range(1, self.count):
            source = lax.rem(self.me + k, self.count)
            self.copy(k, source).wait_recv()
        for k in range(1, self.count):
            self.copy(k, self.me).wait_send()
        return jnp.sum(self.slots[...], axis=0)


def kernel(
    geo,
    spectra_ref,
    mask_ref,
    delay_ref,
    out_ref,
    x,
    gram,
    stat_y,
    stat_z,
    power_y,
    power_z,
    table_v,
    table,
    thin,
    buf_b,
    buf_c,
    buf_d,
    got,
    best,
    load_sem,
    table_sem,
    halo_send,
    halo_recv,
    ring_send,
    ring_recv,
    swap_send,
    swap_recv,
    own_sem,
):
    tiles, own, rows = geo.tiles, geo.own, geo.rows
    sub_index = lax.axis_index("sub")
    tm_index = lax.axis_index("tm")
    z_index, y_index = tm_index // geo.ny, lax.rem(tm_index, geo.ny)
    position = reversed_bits(sub_index, geo.cross_levels)
    not_first = tm_index > 0
    not_last = tm_index < geo.ny * geo.nz - 1

    def along_y(peer):
        return {"tm": z_index * geo.ny + peer}

    def along_z(peer):
        return {"tm": peer * geo.ny + y_index}

    own_first = LEFT * LANES
    right_first = (LEFT + own) * LANES
    chunk = geo.samples // 4
    loads = []
    for i in range(4):
        loads.append(
            pltpu.make_async_copy(
                spectra_ref.at[:, pl.ds(i * chunk, chunk)],
                x.at[:, pl.ds(own_first + i * chunk, chunk)],
                load_sem.at[i],
            )
        )
        loads[-1].start()

    barrier = pltpu.get_barrier_semaphore()
    for k in range(1, geo.ny):
        pl.semaphore_signal(barrier, inc=1, device_id=along_y(lax.rem(y_index + k, geo.ny)), device_id_type=MESH)
    for k in range(1, geo.nz):
        pl.semaphore_signal(barrier, inc=1, device_id=along_z(lax.rem(z_index + k, geo.nz)), device_id_type=MESH)
    for k in range(1, geo.n_sub):
        pl.semaphore_signal(
            barrier, inc=1, device_id={"sub": lax.rem(sub_index + k, geo.n_sub)}, device_id_type=MESH
        )

    n_tm = geo.ny * geo.nz
    for k in (1, n_tm - 1):
        pl.semaphore_signal(barrier, inc=1, device_id={"tm": lax.rem(tm_index + k, n_tm)}, device_id_type=MESH)
    pl.semaphore_wait(barrier, geo.ny + geo.nz + geo.n_sub - 1)

    def to_prev():
        return remote(
            spectra_ref.at[:, pl.ds(0, RIGHT * LANES)],
            x.at[:, pl.ds(right_first, RIGHT * LANES)],
            halo_send.at[0],
            halo_recv.at[0],
            {"tm": tm_index - 1},
        )

    def to_next():
        return remote(
            spectra_ref.at[:, pl.ds(geo.samples - LEFT * LANES, LEFT * LANES)],
            x.at[:, pl.ds(0, LEFT * LANES)],
            halo_send.at[1],
            halo_recv.at[1],
            {"tm": tm_index + 1},
        )

    @pl.when(not_first)
    def _():
        to_prev().start()

    @pl.when(not_last)
    def _():
        to_next().start()

    sums = jnp.zeros((8, geo.channels), F32)
    for i in range(4):
        loads[i].wait()
        part = x[:, pl.ds(own_first + i * chunk, chunk)]
        nt = (((1,), (1,)), ((), ()))
        square = lax.dot_general(part, part, nt, preferred_element_type=F32)
        if i == 0:
            gram[...] = square
        else:
            gram[...] += square
        sums = sums + lax.dot_general(jnp.ones((8, chunk), BF16), part, nt, preferred_element_type=F32)
    diagonal = iota((geo.channels, geo.channels), 0) == iota((geo.channels, geo.channels), 1)
    squares = jnp.sum(jnp.where(diagonal, gram[...], 0.0), axis=0, keepdims=True)
    half = geo.channels // 2
    stats = jnp.concatenate(
        [sums[0:1, :half], sums[0:1, half:], squares[:, :half], squares[:, half:], jnp.zeros((4, half), F32)], axis=0
    )
    over_y = Ring(stat_y, y_index, geo.ny, along_y, ring_send.at[0], ring_recv.at[0])
    over_z = Ring(stat_z, z_index, geo.nz, along_z, ring_send.at[1], ring_recv.at[1])
    over_y.start(stats)

    table_v[...] = delay_table(geo, position, sub_index, delay_ref)
    table_copy = pltpu.make_async_copy(table_v, table, table_sem)
    table_copy.start()

    over_z.start(over_y.total())

    @pl.when(jnp.logical_not(not_first))
    def _():
        x[:, pl.ds(0, LEFT * LANES)] = jnp.zeros((geo.channels, LEFT * LANES), BF16)

    @pl.when(jnp.logical_not(not_last))
    def _():
        x[:, pl.ds(right_first, RIGHT * LANES)] = jnp.zeros((geo.channels, RIGHT * LANES), BF16)

    totals = over_z.total()
    table_copy.wait()
    total_time = geo.samples * geo.ny * geo.nz
    centre = jnp.concatenate([totals[0:1], totals[1:2]], axis=1) / total_time
    power = jnp.concatenate([totals[2:3], totals[3:4]], axis=1) / total_time
    spread = lax.rsqrt(power - centre * centre + 1e-05)
    weight = spread * mask_ref[...].astype(F32)
    bands = geo.channels // 8
    member = iota((bands, geo.channels), 1) // 8 == iota((bands, geo.channels), 0)
    gain = jnp.where(member, weight, 0.0)
    gain_1 = gain.astype(BF16)
    rest = gain - gain_1.astype(F32)
    gain_2 = rest.astype(BF16)
    gain_3 = (rest - gain_2.astype(F32)).astype(BF16)
    gains = jnp.concatenate([gain_1, gain_2, gain_3], axis=0)
    offset = -jnp.sum(gain * centre, axis=1, keepdims=True)

    def normalise(first, count, shift):
        sample = jnp.dot(gains, x[:, pl.ds(first * LANES, count * LANES)], preferred_element_type=F32)
        value = sample[:bands] + sample[bands : 2 * bands] + sample[2 * bands :] + shift
        for g in range(bands // 8):
            for j in range(count):
                thin[pl.ds(8 * g * tiles + first + j, 8, stride=tiles), :] = value[
                    8 * g : 8 * g + 8, j * LANES : (j + 1) * LANES
                ]

    for i in range(own // 4):
        normalise(LEFT + 4 * i, 4, offset)

    @pl.when(not_first)
    def _():
        to_prev().wait_send()
        to_next().wait_recv()

    @pl.when(not_last)
    def _():
        to_next().wait_send()
        to_prev().wait_recv()

    normalise(0, LEFT, jnp.where(not_first, offset, 0.0))
    normalise(LEFT + own, RIGHT, jnp.where(not_last, offset, 0.0))

    first_merge(geo, thin, buf_b, table)
    buffers = [buf_b, buf_c]
    for level in range(5, geo.local_levels + 1):
        src, dst = buffers
        merge(geo, src, dst, table, level, 2 ** (level - 3))
        buffers = [dst, src]
    local_plane, spare = buffers

    share = rows // geo.n_sub * tiles

    def swap(k, slot):
        peer = lax.rem(sub_index + k, geo.n_sub)
        return remote(
            local_plane.at[pl.ds(peer * share, share), :],
            got.at[pl.ds(slot * share, share), :],
            swap_send.at[k],
            swap_recv.at[slot],
            {"sub": peer},
        )

    for k in range(1, geo.n_sub):
        swap(k, position).start()
    keep = pltpu.make_async_copy(
        local_plane.at[pl.ds(sub_index * share, share), :], got.at[pl.ds(position * share, share), :], own_sem
    )
    keep.start()
    for k in range(1, geo.n_sub):
        source = lax.rem(sub_index + k, geo.n_sub)
        swap(k, reversed_bits(source, geo.cross_levels)).wait_recv()
    for k in range(1, geo.n_sub):
        swap(k, position).wait_send()
    keep.wait()

    src, dst, other = got, spare, buf_d
    for up in range(1, geo.cross_levels + 1):
        level = geo.local_levels + up
        merge(geo, src, dst, table, level, rows // geo.n_sub * 2 ** (up - 1), wide=level >= 11)
        src, dst, other = dst, other, dst
    final = src

    lane = iota((8, LANES), 1)

    def group_tile(g, j):
        return final[pl.ds(8 * g * tiles + j, 8, stride=tiles), :]

    def group_power(g, packed):
        total = jnp.zeros((8, LANES), F32)
        for j in range(LEFT, LEFT + own):
            tile = group_tile(g, j)
            total = total + tile * tile
        return jnp.where(lane == g, jnp.sum(total, axis=1, keepdims=True), packed)

    packed = lax.fori_loop(0, rows // 8, group_power, jnp.zeros((8, LANES), F32))
    over_y = Ring(power_y, y_index, geo.ny, along_y, ring_send.at[2], ring_recv.at[2])
    over_z = Ring(power_z, z_index, geo.nz, along_z, ring_send.at[3], ring_recv.at[3])
    over_y.start(packed)

    def group_best(g, carry):
        box = [jnp.where(not_first, group_tile(g, 0), 0.0)]
        box += [group_tile(g, j) for j in range(1, LEFT + own)]
        for section in range(WIDTHS):
            if section > 0:
                lag = 2 ** (section - 1)
                near = lane < LANES - lag
                for j in range(LEFT + own - 1, -1, -1):
                    mixed = jnp.where(near, box[j], box[max(j - 1, 0)])
                    box[j] = box[j] + pltpu.roll(mixed, lag, 1)
            found = [jnp.maximum(box[LEFT + 2 * b], box[LEFT + 2 * b + 1]) for b in range(own // 2)]
            step = 1
            while len(found) > 1:
                even = (lane & step) == 0
                found = [
                    jnp.maximum(jnp.where(even, a, b), pltpu.roll(jnp.where(even, b, a), step, 1))
                    for a, b in zip(found[::2], found[1::2])
                ]
                step *= 2
            largest = found[0]
            while step < LANES:
                largest = jnp.maximum(largest, pltpu.roll(largest, step, 1))
                step *= 2
            best[pl.ds(pl.multiple_of(section * rows + 8 * g, 8), 8), :] = largest
        return carry

    groups = rows // 8
    lax.fori_loop(0, groups // 2, group_best, 0)
    over_z.start(over_y.total())
    lax.fori_loop(groups // 2, groups, group_best, 0)
    mean_power = over_z.total() / total_time
    inverse = 1.0 / jnp.sqrt(mean_power + 1e-06)
    for g in range(groups):
        scale = jnp.sum(jnp.where(lane == g, inverse, 0.0), axis=1, keepdims=True)
        for section in range(WIDTHS):
            value = best[section * rows + 8 * g : section * rows + 8 * g + 8, :]
            buf_d[pl.ds(8 * WIDTHS * g + section, 8, stride=WIDTHS), :] = value * (
                scale * (1.0 / math.sqrt(2**section))
            )
    out_ref[...] = buf_d[0 : rows * WIDTHS, 0 : own // 2]


class Geometry:
    pass


def local(mesh, spectra, chan_mask, delay_step):
    geo = Geometry()
    geo.n_sub = mesh.shape["sub"]
    n_tm = mesh.shape["tm"]
    geo.ny = 4 if n_tm % 4 == 0 else n_tm
    geo.nz = n_tm // geo.ny
    geo.channels, geo.samples = spectra.shape
    geo.cross_levels = geo.n_sub.bit_length() - 1
    geo.local_levels = geo.channels.bit_length() - 1
    geo.rows = geo.channels // 4
    geo.own = geo.samples // LANES
    geo.tiles = LEFT + geo.own + RIGHT
    tall = geo.rows * geo.tiles + 64
    dma = pltpu.SemaphoreType.DMA
    slots = max(geo.ny, geo.nz)
    best = pl.pallas_call(
        functools.partial(kernel, geo),
        out_shape=jax.ShapeDtypeStruct((geo.rows * WIDTHS, geo.own // 2), F32),
        in_specs=[
            pl.BlockSpec(memory_space=pl.ANY),
            pl.BlockSpec(memory_space=pltpu.VMEM),
            pl.BlockSpec(memory_space=pltpu.VMEM),
        ],
        out_specs=pl.BlockSpec(memory_space=pltpu.VMEM),
        scratch_shapes=[
            pltpu.VMEM((geo.channels, geo.tiles * LANES), BF16),
            pltpu.VMEM((geo.channels, geo.channels), F32),
            pltpu.VMEM((geo.ny, 8, LANES), F32),
            pltpu.VMEM((geo.nz, 8, LANES), F32),
            pltpu.VMEM((geo.ny, 8, LANES), F32),
            pltpu.VMEM((geo.nz, 8, LANES), F32),
            pltpu.VMEM((8, LANES), I32),
            pltpu.SMEM((8, LANES), I32),
            pltpu.VMEM((geo.rows // 2 * geo.tiles + 64, LANES), F32),
            pltpu.VMEM((tall, LANES), F32),
            pltpu.VMEM((tall, LANES), F32),
            pltpu.VMEM((tall, LANES), F32),
            pltpu.VMEM((tall, LANES), F32),
            pltpu.VMEM((geo.rows * WIDTHS, LANES), F32),
            dma((4,)),
            dma(()),
            dma((2,)),
            dma((2,)),
            dma((4, slots)),
            dma((4, slots)),
            dma((geo.n_sub,)),
            dma((geo.n_sub,)),
            dma(()),
        ],
        compiler_params=pltpu.CompilerParams(collective_id=0, has_side_effects=True, vmem_limit_bytes=48 * 2**20),
        name="dedisperse",
    )(spectra, chan_mask.reshape(1, geo.channels), delay_step.reshape(-1, LANES))
    return best.reshape(geo.rows, WIDTHS, geo.own // 2)


def solution(mesh):
    in_specs = (P("sub", "tm"), P("sub"), P())
    out_specs = P("sub", None, "tm")
    return jax.shard_map(
        functools.partial(local, mesh), mesh=mesh, in_specs=in_specs, out_specs=out_specs, check_vma=False
    )
```

time: 1940 us -> 62.5 us (0.03)
  the two profiles are of different devices: /device:TPU:128 before, /device:TPU:1 now
where the time goes in v1:
time: 62.5 us; the launch traced here: 62.3 us
  Pallas kernels  58.6 us (94%)
  local copies, waits for them, and re-layouts  3.73 us (6%)
    pallas_call x1, Pallas kernels, local(): pl.pallas_call(functools.partial(kernel, geo), out_shape=jax.ShapeDtypeSt...  58.6 us
    unnamed x6, local copies, waits for them, and re-layouts  2.97 us

profile of v1, /device:TPU:1, one launch (start us, length us, event | category | flops | bytes accessed | tf_op | source)
XLA Modules:
  0.0 62.3 jit_solution(17800638300949227375)
XLA Ops:
  0.0 0.0 copy-start
  0.0 1.6 %copy-done = bf16[256,4096]{1,0:T(8,128)(2,1)S(1)} copy-done((bf16[256,4096]{1,0:T(8,128)(2,1)S(1)}, bf16[256,4096]{1,0:T(8,128)(2,1)}, u32[]{:S(2)}) %copy-start) | copy-done | bytes 2097176
  1.6 0.0 copy-start.1
  1.6 0.7 %copy-done.1 = s32[2048]{0:T(1024)S(1)} copy-done((s32[2048]{0:T(1024)S(1)}, s32[2048]{0:T(1024)}, u32[]{:S(2)}) %copy-start.1) | copy-done | bytes 8216
  2.3 0.0 copy-start.2
  2.3 0.7 %copy-done.2 = s32[256]{0:T(256)S(1)} copy-done((s32[256]{0:T(256)S(1)}, s32[256]{0:T(256)}, u32[]{:S(2)}) %copy-start.2) | copy-done | bytes 1048
  3.0 58.6 %dedisperse.1 = f32[512,16]{1,0:T(8,128)S(1)} custom-call(bf16[256,4096]{1,0:T(8,128)(2,1)S(1)} %copy-done, s32[1,256]{1,0:T(1,128)S(1)} %bitcast.5, s32[16,128]{1,0:T(8,128)S(1)} %bitcast.4), custom_call_target="tpu_custom_call" | custom-call | tf_op jit(solution)/shard_map/dedisperse/pallas_call | solution.py:452
  61.6 0.8 %copy.4 = f32[64,8,16]{0,2,1:T(8,128)} copy(f32[64,8,16]{2,1,0:T(8,128)S(1)} %bitcast.3) | data formatting | bytes 65536 | tf_op jit(solution)/shard_map/reshape | solution.py:489
Async XLA Ops:
  0.0 1.6 %copy-start = (bf16[256,4096]{1,0:T(8,128)(2,1)S(1)}, bf16[256,4096]{1,0:T(8,128)(2,1)}, u32[]{:S(2)}) copy-start(bf16[256,4096]{1,0:T(8,128)(2,1)} %spectra_ref.1) | copy-start | bytes 6291460
  1.6 0.7 %copy-start.1 = (s32[2048]{0:T(1024)S(1)}, s32[2048]{0:T(1024)}, u32[]{:S(2)}) copy-start(s32[2048]{0:T(1024)} %param.5) | copy-start | bytes 24580
  2.3 0.7 %copy-start.2 = (s32[256]{0:T(256)S(1)}, s32[256]{0:T(256)}, u32[]{:S(2)}) copy-start(s32[256]{0:T(256)} %param.4) | copy-start | bytes 3076

commit v2 on v1

--- a/solution.py
+++ b/solution.py
@@ -17,6 +17,7 @@
 LANES = 128
 LEFT = 1
 RIGHT = 4
+CODE = 32767.0
 SPAN = 40
 
 
@@ -108,7 +109,7 @@
             dst[pl.ds((2 * p + i) * step, SPAN), :] = lower_rows + moved
         return carry
 
-    lax.fori_loop(0, geo.rows // 2, pair, 0, unroll=2)
+    lax.fori_loop(0, geo.rows // 2, pair, 0, unroll=16)
 
 
 def first_merge(geo, src, dst, table):
@@ -127,7 +128,7 @@
             dst[pl.ds((4 * s + i) * step, SPAN), :] = lower_rows + moved
         return carry
 
-    lax.fori_loop(0, geo.rows // 4, band, 0)
+    lax.fori_loop(0, geo.rows // 4, band, 0, unroll=8)
 
 
 class Ring:
@@ -155,11 +156,24 @@
         return jnp.sum(self.slots[...], axis=0)
 
 
+def along(values, index, axis):
+    numbers = lax.GatherDimensionNumbers(
+        offset_dims=(),
+        collapsed_slice_dims=(axis,),
+        start_index_map=(axis,),
+        operand_batching_dims=(1 - axis,),
+        start_indices_batching_dims=(1 - axis,),
+    )
+    return lax.gather(
+        values, index[..., None], numbers, slice_sizes=(1, 1), mode=lax.GatherScatterMode.PROMISE_IN_BOUNDS
+    )
+
+
 def kernel(
     geo,
     spectra_ref,
-    mask_ref,
-    delay_ref,
+    mask_hbm,
+    delay_hbm,
     out_ref,
     x,
     gram,
@@ -170,12 +184,17 @@
     table_v,
     table,
     thin,
-    buf_b,
-    buf_c,
-    buf_d,
+    plane,
+    other,
+    coded,
+    coded_scale,
     got,
+    got_scale,
     best,
+    mask_ref,
+    delay_ref,
     load_sem,
+    small_sem,
     table_sem,
     halo_send,
     halo_recv,
@@ -185,19 +204,33 @@
     swap_recv,
     own_sem,
 ):
-    tiles, own, rows = geo.tiles, geo.own, geo.rows
+    tiles, own = geo.tiles, geo.own
     sub_index = lax.axis_index("sub")
     tm_index = lax.axis_index("tm")
     z_index, y_index = tm_index // geo.ny, lax.rem(tm_index, geo.ny)
-    position = reversed_bits(sub_index, geo.cross_levels)
+    position = reversed_bits(sub_index, 3)
+    n_tm = geo.ny * geo.nz
     not_first = tm_index > 0
-    not_last = tm_index < geo.ny * geo.nz - 1
+    not_last = tm_index < n_tm - 1
+    lane = iota((8, LANES), 1)
 
     def along_y(peer):
         return {"tm": z_index * geo.ny + peer}
 
     def along_z(peer):
         return {"tm": peer * geo.ny + y_index}
+
+    barrier = pltpu.get_barrier_semaphore()
+    for k in range(1, geo.ny):
+        pl.semaphore_signal(barrier, inc=1, device_id=along_y(lax.rem(y_index + k, geo.ny)), device_id_type=MESH)
+    for k in range(1, geo.nz):
+        pl.semaphore_signal(barrier, inc=1, device_id=along_z(lax.rem(z_index + k, geo.nz)), device_id_type=MESH)
+    for k in range(1, geo.n_sub):
+        pl.semaphore_signal(
+            barrier, inc=1, device_id={"sub": lax.rem(sub_index + k, geo.n_sub)}, device_id_type=MESH
+        )
+    for k in (1, n_tm - 1):
+        pl.semaphore_signal(barrier, inc=1, device_id={"tm": lax.rem(tm_index + k, n_tm)}, device_id_type=MESH)
 
     own_first = LEFT * LANES
     right_first = (LEFT + own) * LANES
@@ -212,53 +245,18 @@
             )
         )
         loads[-1].start()
-
-    barrier = pltpu.get_barrier_semaphore()
-    for k in range(1, geo.ny):
-        pl.semaphore_signal(barrier, inc=1, device_id=along_y(lax.rem(y_index + k, geo.ny)), device_id_type=MESH)
-    for k in range(1, geo.nz):
-        pl.semaphore_signal(barrier, inc=1, device_id=along_z(lax.rem(z_index + k, geo.nz)), device_id_type=MESH)
-    for k in range(1, geo.n_sub):
-        pl.semaphore_signal(
-            barrier, inc=1, device_id={"sub": lax.rem(sub_index + k, geo.n_sub)}, device_id_type=MESH
-        )
-
-    n_tm = geo.ny * geo.nz
-    for k in (1, n_tm - 1):
-        pl.semaphore_signal(barrier, inc=1, device_id={"tm": lax.rem(tm_index + k, n_tm)}, device_id_type=MESH)
-    pl.semaphore_wait(barrier, geo.ny + geo.nz + geo.n_sub - 1)
-
-    def to_prev():
-        return remote(
-            spectra_ref.at[:, pl.ds(0, RIGHT * LANES)],
-            x.at[:, pl.ds(right_first, RIGHT * LANES)],
-            halo_send.at[0],
-            halo_recv.at[0],
-            {"tm": tm_index - 1},
-        )
-
-    def to_next():
-        return remote(
-            spectra_ref.at[:, pl.ds(geo.samples - LEFT * LANES, LEFT * LANES)],
-            x.at[:, pl.ds(0, LEFT * LANES)],
-            halo_send.at[1],
-            halo_recv.at[1],
-            {"tm": tm_index + 1},
-        )
-
-    @pl.when(not_first)
-    def _():
-        to_prev().start()
-
-    @pl.when(not_last)
-    def _():
-        to_next().start()
+    small = [
+        pltpu.make_async_copy(mask_hbm, mask_ref, small_sem.at[0]),
+        pltpu.make_async_copy(delay_hbm, delay_ref, small_sem.at[1]),
+    ]
+    for copy in small:
+        copy.start()
 
     sums = jnp.zeros((8, geo.channels), F32)
+    nt = (((1,), (1,)), ((), ()))
     for i in range(4):
         loads[i].wait()
         part = x[:, pl.ds(own_first + i * chunk, chunk)]
-        nt = (((1,), (1,)), ((), ()))
         square = lax.dot_general(part, part, nt, preferred_element_type=F32)
         if i == 0:
             gram[...] = square
@@ -271,27 +269,55 @@
     stats = jnp.concatenate(
         [sums[0:1, :half], sums[0:1, half:], squares[:, :half], squares[:, half:], jnp.zeros((4, half), F32)], axis=0
     )
+    pl.semaphore_wait(barrier, geo.ny + geo.nz + geo.n_sub - 1)
     over_y = Ring(stat_y, y_index, geo.ny, along_y, ring_send.at[0], ring_recv.at[0])
     over_z = Ring(stat_z, z_index, geo.nz, along_z, ring_send.at[1], ring_recv.at[1])
     over_y.start(stats)
 
+    def to_prev():
+        return remote(
+            spectra_ref.at[:, pl.ds(0, RIGHT * LANES)],
+            x.at[:, pl.ds(right_first, RIGHT * LANES)],
+            halo_send.at[0],
+            halo_recv.at[0],
+            {"tm": tm_index - 1},
+        )
+
+    def to_next():
+        return remote(
+            spectra_ref.at[:, pl.ds(geo.samples - LEFT * LANES, LEFT * LANES)],
+            x.at[:, pl.ds(0, LEFT * LANES)],
+            halo_send.at[1],
+            halo_recv.at[1],
+            {"tm": tm_index + 1},
+        )
+
+    @pl.when(not_first)
+    def _():
+        to_prev().start()
+
+    @pl.when(not_last)
+    def _():
+        to_next().start()
+
+    @pl.when(jnp.logical_not(not_first))
+    def _():
+        x[:, pl.ds(0, LEFT * LANES)] = jnp.zeros((geo.channels, LEFT * LANES), BF16)
+
+    @pl.when(jnp.logical_not(not_last))
+    def _():
+        x[:, pl.ds(right_first, RIGHT * LANES)] = jnp.zeros((geo.channels, RIGHT * LANES), BF16)
+
+    for copy in small:
+        copy.wait()
     table_v[...] = delay_table(geo, position, sub_index, delay_ref)
     table_copy = pltpu.make_async_copy(table_v, table, table_sem)
     table_copy.start()
-
     over_z.start(over_y.total())
-
-    @pl.when(jnp.logical_not(not_first))
-    def _():
-        x[:, pl.ds(0, LEFT * LANES)] = jnp.zeros((geo.channels, LEFT * LANES), BF16)
-
-    @pl.when(jnp.logical_not(not_last))
-    def _():
-        x[:, pl.ds(right_first, RIGHT * LANES)] = jnp.zeros((geo.channels, RIGHT * LANES), BF16)
 
     totals = over_z.total()
     table_copy.wait()
-    total_time = geo.samples * geo.ny * geo.nz
+    total_time = geo.samples * n_tm
     centre = jnp.concatenate([totals[0:1], totals[1:2]], axis=1) / total_time
     power = jnp.concatenate([totals[2:3], totals[3:4]], axis=1) / total_time
     spread = lax.rsqrt(power - centre * centre + 1e-05)
@@ -331,47 +357,88 @@
     normalise(0, LEFT, jnp.where(not_first, offset, 0.0))
     normalise(LEFT + own, RIGHT, jnp.where(not_last, offset, 0.0))
 
-    first_merge(geo, thin, buf_b, table)
-    buffers = [buf_b, buf_c]
+    first_merge(geo, thin, plane, table)
+    src, dst = plane, other
     for level in range(5, geo.local_levels + 1):
-        src, dst = buffers
         merge(geo, src, dst, table, level, 2 ** (level - 3))
-        buffers = [dst, src]
-    local_plane, spare = buffers
-
-    share = rows // geo.n_sub * tiles
-
-    def swap(k, slot):
+        src, dst = dst, src
+
+    pairs = (tiles + 1) // 2
+
+    def swap(k, peer, slot):
+        return (
+            remote(coded.at[peer], got.at[slot], swap_send.at[0, k], swap_recv.at[0, slot], {"sub": peer}),
+            remote(
+                coded_scale.at[peer], got_scale.at[slot], swap_send.at[1, k], swap_recv.at[1, slot], {"sub": peer}
+            ),
+        )
+
+    def keep():
+        return (
+            pltpu.make_async_copy(coded.at[sub_index], got.at[position], own_sem.at[0]),
+            pltpu.make_async_copy(coded_scale.at[sub_index], got_scale.at[position], own_sem.at[1]),
+        )
+
+    def piece(block, j):
+        return pl.ds(pl.multiple_of(8 * (block * tiles + j), 8), 8)
+
+    def column(j):
+        return slice(j * LANES, (j + 1) * LANES)
+
+    def send(k, carry):
         peer = lax.rem(sub_index + k, geo.n_sub)
-        return remote(
-            local_plane.at[pl.ds(peer * share, share), :],
-            got.at[pl.ds(slot * share, share), :],
-            swap_send.at[k],
-            swap_recv.at[slot],
-            {"sub": peer},
-        )
-
-    for k in range(1, geo.n_sub):
-        swap(k, position).start()
-    keep = pltpu.make_async_copy(
-        local_plane.at[pl.ds(sub_index * share, share), :], got.at[pl.ds(position * share, share), :], own_sem
-    )
-    keep.start()
-    for k in range(1, geo.n_sub):
-        source = lax.rem(sub_index + k, geo.n_sub)
-        swap(k, reversed_bits(source, geo.cross_levels)).wait_recv()
-    for k in range(1, geo.n_sub):
-        swap(k, position).wait_send()
-    keep.wait()
-
-    src, dst, other = got, spare, buf_d
-    for up in range(1, geo.cross_levels + 1):
-        level = geo.local_levels + up
-        merge(geo, src, dst, table, level, rows // geo.n_sub * 2 ** (up - 1), wide=level >= 11)
-        src, dst, other = dst, other, dst
-    final = src
-
-    lane = iota((8, LANES), 1)
+        scales = jnp.zeros((8, LANES), F32)
+        for j in range(pairs):
+            one = src[piece(peer, j), :]
+            two = src[piece(peer, min(j + pairs, tiles - 1)), :]
+            largest = jnp.max(jnp.maximum(jnp.abs(one), jnp.abs(two)), axis=1, keepdims=True)
+            largest = jnp.maximum(largest, 1e-30)
+            factor = CODE / largest
+            code = jnp.concatenate([one * factor, two * factor], axis=0)
+            coded[pl.ds(peer, 1), :, column(j)] = jnp.round(code).astype(I32).astype(jnp.int16)[None]
+            scales = jnp.where(lane == j, largest * (1.0 / CODE), scales)
+        coded_scale[pl.ds(peer, 1)] = scales[None]
+
+        @pl.when(k < geo.n_sub)
+        def _():
+            for copy in swap(k, peer, position):
+                copy.start()
+
+        @pl.when(k == geo.n_sub)
+        def _():
+            for copy in keep():
+                copy.start()
+
+        return carry
+
+    lax.fori_loop(1, geo.n_sub + 1, send, 0)
+
+    def decode(slot):
+        scales = jnp.reshape(got_scale[pl.ds(slot, 1)], (8, LANES))
+        for j in range(pairs):
+            code = jnp.reshape(got[pl.ds(slot, 1), :, column(j)], (16, LANES)).astype(F32)
+            scale = along(scales, jnp.full((8, LANES), j, I32), 1)
+            dst[piece(slot, j), :] = code[0:8] * scale
+            if j + pairs < tiles:
+                dst[piece(slot, j + pairs), :] = code[8:16] * scale
+
+    def receive(k, carry):
+        source = lax.rem(sub_index - k + geo.n_sub, geo.n_sub)
+        slot = reversed_bits(source, 3)
+        for copy in swap(k, source, slot):
+            copy.wait_recv()
+        decode(slot)
+        return carry
+
+    for copy in keep():
+        copy.wait()
+    decode(position)
+    lax.fori_loop(1, geo.n_sub, receive, 0)
+
+    for level in range(9, 12):
+        src, dst = dst, src
+        merge(geo, src, dst, table, level, 2 ** (level - 6), wide=level == 11)
+    final = dst
 
     def group_tile(g, j):
         return final[pl.ds(8 * g * tiles + j, 8, stride=tiles), :]
@@ -383,7 +450,7 @@
             total = total + tile * tile
         return jnp.where(lane == g, jnp.sum(total, axis=1, keepdims=True), packed)
 
-    packed = lax.fori_loop(0, rows // 8, group_power, jnp.zeros((8, LANES), F32))
+    packed = lax.fori_loop(0, 8, group_power, jnp.zeros((8, LANES), F32), unroll=4)
     over_y = Ring(power_y, y_index, geo.ny, along_y, ring_send.at[2], ring_recv.at[2])
     over_z = Ring(power_z, z_index, geo.nz, along_z, ring_send.at[3], ring_recv.at[3])
     over_y.start(packed)
@@ -391,6 +458,7 @@
     def group_best(g, carry):
         box = [jnp.where(not_first, group_tile(g, 0), 0.0)]
         box += [group_tile(g, j) for j in range(1, LEFT + own)]
+        kept = jnp.zeros((8, LANES), F32)
         for section in range(WIDTHS):
             if section > 0:
                 lag = 2 ** (section - 1)
@@ -411,23 +479,22 @@
             while step < LANES:
                 largest = jnp.maximum(largest, pltpu.roll(largest, step, 1))
                 step *= 2
-            best[pl.ds(pl.multiple_of(section * rows + 8 * g, 8), 8), :] = largest
+            kept = jnp.where((lane >> 4) == section, largest * (1.0 / math.sqrt(2**section)), kept)
+        best[pl.ds(pl.multiple_of(8 * g, 8), 8), :] = kept
         return carry
 
-    groups = rows // 8
-    lax.fori_loop(0, groups // 2, group_best, 0)
+    lax.fori_loop(0, 4, group_best, 0)
     over_z.start(over_y.total())
-    lax.fori_loop(groups // 2, groups, group_best, 0)
+    lax.fori_loop(4, 8, group_best, 0)
+    for k in range(1, geo.n_sub):
+        for copy in swap(k, lax.rem(sub_index + k, geo.n_sub), position):
+            copy.wait_send()
     mean_power = over_z.total() / total_time
     inverse = 1.0 / jnp.sqrt(mean_power + 1e-06)
-    for g in range(groups):
+    for g in range(8):
         scale = jnp.sum(jnp.where(lane == g, inverse, 0.0), axis=1, keepdims=True)
-        for section in range(WIDTHS):
-            value = best[section * rows + 8 * g : section * rows + 8 * g + 8, :]
-            buf_d[pl.ds(8 * WIDTHS * g + section, 8, stride=WIDTHS), :] = value * (
-                scale * (1.0 / math.sqrt(2**section))
-            )
-    out_ref[...] = buf_d[0 : rows * WIDTHS, 0 : own // 2]
+        best[8 * g : 8 * g + 8, :] = best[8 * g : 8 * g + 8, :] * scale
+    out_ref[...] = best[...].T
 
 
 class Geometry:
@@ -438,28 +505,25 @@
     geo = Geometry()
     geo.n_sub = mesh.shape["sub"]
     n_tm = mesh.shape["tm"]
-    geo.ny = 4 if n_tm % 4 == 0 else n_tm
+    geo.ny = 4
     geo.nz = n_tm // geo.ny
     geo.channels, geo.samples = spectra.shape
-    geo.cross_levels = geo.n_sub.bit_length() - 1
-    geo.local_levels = geo.channels.bit_length() - 1
-    geo.rows = geo.channels // 4
     geo.own = geo.samples // LANES
     geo.tiles = LEFT + geo.own + RIGHT
-    tall = geo.rows * geo.tiles + 64
+    assert (geo.n_sub, geo.channels, geo.own, geo.ny * geo.nz) == (8, 256, 32, n_tm)
     dma = pltpu.SemaphoreType.DMA
     slots = max(geo.ny, geo.nz)
+    width = geo.tiles * LANES
+    geo.rows, geo.local_levels, geo.cross_levels = 64, 8, 3
+    pairs = (geo.tiles + 1) // 2
+    anywhere = pl.BlockSpec(memory_space=pl.ANY)
     best = pl.pallas_call(
         functools.partial(kernel, geo),
-        out_shape=jax.ShapeDtypeStruct((geo.rows * WIDTHS, geo.own // 2), F32),
-        in_specs=[
-            pl.BlockSpec(memory_space=pl.ANY),
-            pl.BlockSpec(memory_space=pltpu.VMEM),
-            pl.BlockSpec(memory_space=pltpu.VMEM),
-        ],
+        out_shape=jax.ShapeDtypeStruct((WIDTHS * geo.own // 2, 64), F32),
+        in_specs=[anywhere, anywhere, anywhere],
         out_specs=pl.BlockSpec(memory_space=pltpu.VMEM),
         scratch_shapes=[
-            pltpu.VMEM((geo.channels, geo.tiles * LANES), BF16),
+            pltpu.VMEM((geo.channels, width), BF16),
             pltpu.VMEM((geo.channels, geo.channels), F32),
             pltpu.VMEM((geo.ny, 8, LANES), F32),
             pltpu.VMEM((geo.nz, 8, LANES), F32),
@@ -467,26 +531,31 @@
             pltpu.VMEM((geo.nz, 8, LANES), F32),
             pltpu.VMEM((8, LANES), I32),
             pltpu.SMEM((8, LANES), I32),
-            pltpu.VMEM((geo.rows // 2 * geo.tiles + 64, LANES), F32),
-            pltpu.VMEM((tall, LANES), F32),
-            pltpu.VMEM((tall, LANES), F32),
-            pltpu.VMEM((tall, LANES), F32),
-            pltpu.VMEM((tall, LANES), F32),
-            pltpu.VMEM((geo.rows * WIDTHS, LANES), F32),
+            pltpu.VMEM((32 * geo.tiles + 64, LANES), F32),
+            pltpu.VMEM((64 * geo.tiles + 64, LANES), F32),
+            pltpu.VMEM((64 * geo.tiles + 64, LANES), F32),
+            pltpu.VMEM((8, 16, pairs * LANES), jnp.int16),
+            pltpu.VMEM((8, 8, LANES), F32),
+            pltpu.VMEM((8, 16, pairs * LANES), jnp.int16),
+            pltpu.VMEM((8, 8, LANES), F32),
+            pltpu.VMEM((64, LANES), F32),
+            pltpu.VMEM((1, geo.channels), I32),
+            pltpu.VMEM((16, LANES), I32),
             dma((4,)),
+            dma((2,)),
             dma(()),
             dma((2,)),
             dma((2,)),
             dma((4, slots)),
             dma((4, slots)),
-            dma((geo.n_sub,)),
-            dma((geo.n_sub,)),
-            dma(()),
+            dma((2, geo.n_sub)),
+            dma((2, geo.n_sub)),
+            dma((2,)),
         ],
-        compiler_params=pltpu.CompilerParams(collective_id=0, has_side_effects=True, vmem_limit_bytes=48 * 2**20),
+        compiler_params=pltpu.CompilerParams(collective_id=0, has_side_effects=True, vmem_limit_bytes=62 * 2**20),
         name="dedisperse",
-    )(spectra, chan_mask.reshape(1, geo.channels), delay_step.reshape(-1, LANES))
-    return best.reshape(geo.rows, WIDTHS, geo.own // 2)
+    )(spectra, chan_mask.reshape(1, geo.channels), delay_step.reshape(16, LANES))
+    return best.reshape(WIDTHS, geo.own // 2, 64).transpose(2, 0, 1)
 
 
 def solution(mesh):

time: 62.5 us -> 43.9 us (0.70)
  Pallas kernels: 58.6 us -> 42.2 us
  local copies, waits for them, and re-layouts: 3.73 us -> 1.47 us
    pallas_call x1, Pallas kernels: 58.6 us -> 42.2 us  [local(): pl.pallas_call(functools.partial(kernel, geo), out_shape=jax.ShapeDtypeSt...]
    unnamed x6 -> x1, local copies, waits for them, and re-layouts: 2.97 us -> 1.47 us
    reshape x1 -> x0, local copies, waits for them, and re-layouts: 0.77 us -> none  [local(): return best.reshape(geo.rows, WIDTHS, geo.own // 2)]
where the time goes in v2:
time: 43.9 us; the launch traced here: 43.7 us
  Pallas kernels  42.2 us (96%)
  local copies, waits for them, and re-layouts  1.47 us (3%)
    pallas_call x1, Pallas kernels, local(): pl.pallas_call(functools.partial(kernel, geo), out_shape=jax.ShapeDtypeSt...  42.2 us
    unnamed x1, local copies, waits for them, and re-layouts  1.47 us

profile of v2, /device:TPU:1, one launch (start us, length us, event | category | flops | bytes accessed | tf_op | source)
XLA Modules:
  0.0 43.7 jit_solution(4751569727041547556)
XLA Ops:
  0.0 42.2 %dedisperse.1 = f32[128,64]{1,0:T(8,128)} custom-call(bf16[256,4096]{1,0:T(8,128)(2,1)} %spectra_ref.1, s32[1,256]{1,0:T(1,128)} %bitcast.7, s32[16,128]{1,0:T(8,128)} %bitcast.6), custom_call_target="tpu_custom_call" | custom-call | tf_op jit(solution)/shard_map/dedisperse/pallas_call | solution.py:520
  42.2 1.5 %copy.5 = f32[64,8,16]{0,2,1:T(8,128)} copy(f32[64,8,16]{0,2,1:T(8,128)} %bitcast.5) | data formatting | bytes 65536

commit v3 on v2

--- a/solution.py
+++ b/solution.py
@@ -17,7 +17,6 @@
 LANES = 128
 LEFT = 1
 RIGHT = 4
-CODE = 32767.0
 SPAN = 40
 
 
@@ -85,50 +84,40 @@
     return jnp.concatenate([table, table], axis=1)
 
 
-def merge(geo, src, dst, table, level, fan, wide=False):
+def move_rows(geo, src, steps, dst, lower, upper, shifts, outs, wide=False):
     lane = iota((SPAN, LANES), 1)
-    step = geo.tiles
-
-    def pair(p, carry):
-        low = p + (p // fan) * fan
-        base = low * step
-        upper = base + fan * step
-        lower_rows = src[pl.ds(base, SPAN), :]
-        if not wide:
-            here = src[pl.ds(upper, SPAN), :]
-            after = src[pl.ds(upper + 1, SPAN), :]
-        for i in range(2):
-            shift = table[level - 4, 2 * p + i]
-            if wide:
-                start = upper + (shift >> 7)
-                shift = shift & (LANES - 1)
-                here = src[pl.ds(start, SPAN), :]
-                after = src[pl.ds(start + 1, SPAN), :]
-            mixed = jnp.where(lane >= shift, here, after)
-            moved = pltpu.roll(mixed, (LANES - shift) & (LANES - 1), 1)
-            dst[pl.ds((2 * p + i) * step, SPAN), :] = lower_rows + moved
-        return carry
-
-    lax.fori_loop(0, geo.rows // 2, pair, 0, unroll=16)
+    from_step, to_step = steps
+    lower_rows = src[pl.ds(lower * from_step, SPAN), :]
+    start = upper * from_step
+    if not wide:
+        here = src[pl.ds(start, SPAN), :]
+        after = src[pl.ds(start + 1, SPAN), :]
+    for shift, out in zip(shifts, outs):
+        if wide:
+            tile = start + (shift >> 7)
+            shift = shift & (LANES - 1)
+            here = src[pl.ds(tile, SPAN), :]
+            after = src[pl.ds(tile + 1, SPAN), :]
+        mixed = jnp.where(lane >= shift, here, after)
+        dst[pl.ds(out * to_step, SPAN), :] = lower_rows + pltpu.roll(mixed, (LANES - shift) & (LANES - 1), 1)
+
+
+def merge(geo, src, dst, table, level, fan, half=None, to_step=SPAN):
+    for s in range(32 // fan):
+        for e in range(fan if half is None else fan // 2):
+            first = e if half is None else half * (fan // 2) + e
+            p = s * fan + first
+            outs = [2 * p, 2 * p + 1]
+            shifts = [table[level - 4, out] for out in outs]
+            low = s * 2 * fan + first
+            move_rows(geo, src, (SPAN, to_step), dst, low, low + fan, shifts, outs, wide=level == 11)
 
 
 def first_merge(geo, src, dst, table):
-    lane = iota((SPAN, LANES), 1)
-    step = geo.tiles
-
-    def band(s, carry):
-        base = 2 * s * step
-        lower_rows = src[pl.ds(base, SPAN), :]
-        here = src[pl.ds(base + step, SPAN), :]
-        after = src[pl.ds(base + step + 1, SPAN), :]
-        for i in range(4):
-            shift = table[0, 4 * s + i]
-            mixed = jnp.where(lane >= shift, here, after)
-            moved = pltpu.roll(mixed, (LANES - shift) & (LANES - 1), 1)
-            dst[pl.ds((4 * s + i) * step, SPAN), :] = lower_rows + moved
-        return carry
-
-    lax.fori_loop(0, geo.rows // 4, band, 0, unroll=8)
+    for s in range(16):
+        outs = [4 * s + i for i in range(4)]
+        shifts = [table[0, out] for out in outs]
+        move_rows(geo, src, (geo.tiles, SPAN), dst, 2 * s, 2 * s + 1, shifts, outs)
 
 
 class Ring:
@@ -185,11 +174,11 @@
     table,
     thin,
     plane,
-    other,
+    left,
+    right,
+    final,
     coded,
-    coded_scale,
     got,
-    got_scale,
     best,
     mask_ref,
     delay_ref,
@@ -213,6 +202,7 @@
     not_first = tm_index > 0
     not_last = tm_index < n_tm - 1
     lane = iota((8, LANES), 1)
+    place = iota((8, LANES), 0)
 
     def along_y(peer):
         return {"tm": z_index * geo.ny + peer}
@@ -267,7 +257,7 @@
     squares = jnp.sum(jnp.where(diagonal, gram[...], 0.0), axis=0, keepdims=True)
     half = geo.channels // 2
     stats = jnp.concatenate(
-        [sums[0:1, :half], sums[0:1, half:], squares[:, :half], squares[:, half:], jnp.zeros((4, half), F32)], axis=0
+        [sums[0:1, :half], sums[0:1, half:], squares[:, :half], squares[:, half:]], axis=0
     )
     pl.semaphore_wait(barrier, geo.ny + geo.nz + geo.n_sub - 1)
     over_y = Ring(stat_y, y_index, geo.ny, along_y, ring_send.at[0], ring_recv.at[0])
@@ -358,87 +348,95 @@
     normalise(LEFT + own, RIGHT, jnp.where(not_last, offset, 0.0))
 
     first_merge(geo, thin, plane, table)
-    src, dst = plane, other
-    for level in range(5, geo.local_levels + 1):
-        merge(geo, src, dst, table, level, 2 ** (level - 3))
-        src, dst = dst, src
-
-    pairs = (tiles + 1) // 2
+    pairs = SPAN // 2
 
     def swap(k, peer, slot):
-        return (
-            remote(coded.at[peer], got.at[slot], swap_send.at[0, k], swap_recv.at[0, slot], {"sub": peer}),
-            remote(
-                coded_scale.at[peer], got_scale.at[slot], swap_send.at[1, k], swap_recv.at[1, slot], {"sub": peer}
-            ),
-        )
-
-    def keep():
-        return (
-            pltpu.make_async_copy(coded.at[sub_index], got.at[position], own_sem.at[0]),
-            pltpu.make_async_copy(coded_scale.at[sub_index], got_scale.at[position], own_sem.at[1]),
-        )
+        return remote(coded.at[peer], got.at[slot], swap_send.at[k], swap_recv.at[slot], {"sub": peer})
+
+    keep = pltpu.make_async_copy(coded.at[sub_index], got.at[position], own_sem)
 
     def piece(block, j):
-        return pl.ds(pl.multiple_of(8 * (block * tiles + j), 8), 8)
+        return pl.ds(pl.multiple_of(8 * (block * SPAN + j), 8), 8)
 
     def column(j):
         return slice(j * LANES, (j + 1) * LANES)
 
-    def send(k, carry):
-        peer = lax.rem(sub_index + k, geo.n_sub)
-        scales = jnp.zeros((8, LANES), F32)
+    def encode(peer):
+        powers = jnp.zeros((8, LANES), F32)
         for j in range(pairs):
-            one = src[piece(peer, j), :]
-            two = src[piece(peer, min(j + pairs, tiles - 1)), :]
+            one = right[piece(peer, j), :]
+            two = right[piece(peer, j + pairs), :]
             largest = jnp.max(jnp.maximum(jnp.abs(one), jnp.abs(two)), axis=1, keepdims=True)
-            largest = jnp.maximum(largest, 1e-30)
-            factor = CODE / largest
+            power = jnp.ceil(jnp.log2(jnp.maximum(largest, 1e-30) * 1.001))
+            factor = jnp.exp2(15.0 - power)
             code = jnp.concatenate([one * factor, two * factor], axis=0)
             coded[pl.ds(peer, 1), :, column(j)] = jnp.round(code).astype(I32).astype(jnp.int16)[None]
-            scales = jnp.where(lane == j, largest * (1.0 / CODE), scales)
-        coded_scale[pl.ds(peer, 1)] = scales[None]
-
-        @pl.when(k < geo.n_sub)
-        def _():
-            for copy in swap(k, peer, position):
-                copy.start()
-
-        @pl.when(k == geo.n_sub)
-        def _():
-            for copy in keep():
-                copy.start()
-
-        return carry
-
-    lax.fori_loop(1, geo.n_sub + 1, send, 0)
+            powers = jnp.where(lane == j, power, powers)
+        powers = jnp.concatenate([powers, powers], axis=0)
+        coded[pl.ds(peer, 1), :, column(pairs)] = powers.astype(I32).astype(jnp.int16)[None]
+
+    near = sub_index // 4
+    far = 1 - near
+    place_in_half = lax.rem(sub_index, 4)
+    for half, first in ((far, 0), (near, 4)):
+        merge(geo, plane, left, table, 5, 4, half)
+        merge(geo, left, right, table, 6, 8, half)
+        merge(geo, right, left, table, 7, 16, half)
+        merge(geo, left, right, table, 8, 32, half)
+
+        def send(k, carry):
+            peer = 4 * half + lax.rem(place_in_half + k, 4)
+            encode(peer)
+            if first == 0:
+                swap(first + k, peer, position).start()
+            else:
+
+                @pl.when(k < 4)
+                def _():
+                    swap(first + k, peer, position).start()
+
+                @pl.when(k == 4)
+                def _():
+                    keep.start()
+
+            return carry
+
+        if first == 0:
+            lax.fori_loop(0, 4, send, 0)
+        else:
+            lax.fori_loop(1, 5, send, 0)
 
     def decode(slot):
-        scales = jnp.reshape(got_scale[pl.ds(slot, 1)], (8, LANES))
+        block = got[pl.ds(slot, 1), :, column(pairs)]
+        scales = jnp.exp2(jnp.reshape(block, (16, LANES)).astype(F32)[0:8] - 15.0)
         for j in range(pairs):
             code = jnp.reshape(got[pl.ds(slot, 1), :, column(j)], (16, LANES)).astype(F32)
             scale = along(scales, jnp.full((8, LANES), j, I32), 1)
-            dst[piece(slot, j), :] = code[0:8] * scale
-            if j + pairs < tiles:
-                dst[piece(slot, j + pairs), :] = code[8:16] * scale
-
-    def receive(k, carry):
-        source = lax.rem(sub_index - k + geo.n_sub, geo.n_sub)
+            plane[piece(slot, j), :] = code[0:8] * scale
+            plane[piece(slot, j + pairs), :] = code[8:16] * scale
+
+    keep.wait()
+    decode(position)
+
+    def receive(source):
         slot = reversed_bits(source, 3)
-        for copy in swap(k, source, slot):
-            copy.wait_recv()
+        swap(0, source, slot).wait_recv()
         decode(slot)
+
+    def receive_far(k, carry):
+        receive(4 * far + lax.rem(place_in_half + 4 - k, 4))
         return carry
 
-    for copy in keep():
-        copy.wait()
-    decode(position)
-    lax.fori_loop(1, geo.n_sub, receive, 0)
-
-    for level in range(9, 12):
-        src, dst = dst, src
-        merge(geo, src, dst, table, level, 2 ** (level - 6), wide=level == 11)
-    final = dst
+    def receive_near(k, carry):
+        receive(4 * near + lax.rem(place_in_half + 4 - k, 4))
+        return carry
+
+    lax.fori_loop(0, 4, receive_far, 0)
+    lax.fori_loop(1, 4, receive_near, 0)
+
+    merge(geo, plane, left, table, 9, 8)
+    merge(geo, left, right, table, 10, 16)
+    merge(geo, right, final, table, 11, 32, to_step=tiles)
 
     def group_tile(g, j):
         return final[pl.ds(8 * g * tiles + j, 8, stride=tiles), :]
@@ -448,12 +446,12 @@
         for j in range(LEFT, LEFT + own):
             tile = group_tile(g, j)
             total = total + tile * tile
-        return jnp.where(lane == g, jnp.sum(total, axis=1, keepdims=True), packed)
-
-    packed = lax.fori_loop(0, 8, group_power, jnp.zeros((8, LANES), F32), unroll=4)
+        return jnp.where(lane == 8 * g + place, jnp.sum(total, axis=1, keepdims=True), packed)
+
+    packed = lax.fori_loop(0, 8, group_power, jnp.zeros((8, LANES), F32), unroll=8)
     over_y = Ring(power_y, y_index, geo.ny, along_y, ring_send.at[2], ring_recv.at[2])
     over_z = Ring(power_z, z_index, geo.nz, along_z, ring_send.at[3], ring_recv.at[3])
-    over_y.start(packed)
+    over_y.start(jnp.sum(packed, axis=0, keepdims=True))
 
     def group_best(g, carry):
         box = [jnp.where(not_first, group_tile(g, 0), 0.0)]
@@ -486,13 +484,12 @@
     lax.fori_loop(0, 4, group_best, 0)
     over_z.start(over_y.total())
     lax.fori_loop(4, 8, group_best, 0)
-    for k in range(1, geo.n_sub):
-        for copy in swap(k, lax.rem(sub_index + k, geo.n_sub), position):
-            copy.wait_send()
+    for k in (0, 1, 2, 3, 5, 6, 7):
+        swap(k, 4 * (far if k < 4 else near) + lax.rem(place_in_half + k, 4), position).wait_send()
     mean_power = over_z.total() / total_time
-    inverse = 1.0 / jnp.sqrt(mean_power + 1e-06)
+    inverse = jnp.broadcast_to(1.0 / jnp.sqrt(mean_power + 1e-06), (8, LANES))
     for g in range(8):
-        scale = jnp.sum(jnp.where(lane == g, inverse, 0.0), axis=1, keepdims=True)
+        scale = jnp.sum(jnp.where(lane == 8 * g + place, inverse, 0.0), axis=1, keepdims=True)
         best[8 * g : 8 * g + 8, :] = best[8 * g : 8 * g + 8, :] * scale
     out_ref[...] = best[...].T
 
@@ -515,7 +512,6 @@
     slots = max(geo.ny, geo.nz)
     width = geo.tiles * LANES
     geo.rows, geo.local_levels, geo.cross_levels = 64, 8, 3
-    pairs = (geo.tiles + 1) // 2
     anywhere = pl.BlockSpec(memory_space=pl.ANY)
     best = pl.pallas_call(
         functools.partial(kernel, geo),
@@ -525,19 +521,19 @@
         scratch_shapes=[
             pltpu.VMEM((geo.channels, width), BF16),
             pltpu.VMEM((geo.channels, geo.channels), F32),
-            pltpu.VMEM((geo.ny, 8, LANES), F32),
-            pltpu.VMEM((geo.nz, 8, LANES), F32),
-            pltpu.VMEM((geo.ny, 8, LANES), F32),
-            pltpu.VMEM((geo.nz, 8, LANES), F32),
+            pltpu.VMEM((geo.ny, 4, LANES), F32),
+            pltpu.VMEM((geo.nz, 4, LANES), F32),
+            pltpu.VMEM((geo.ny, 1, LANES), F32),
+            pltpu.VMEM((geo.nz, 1, LANES), F32),
             pltpu.VMEM((8, LANES), I32),
             pltpu.SMEM((8, LANES), I32),
             pltpu.VMEM((32 * geo.tiles + 64, LANES), F32),
+            pltpu.VMEM((64 * SPAN + 16, LANES), F32),
+            pltpu.VMEM((64 * SPAN + 16, LANES), F32),
+            pltpu.VMEM((64 * SPAN + 16, LANES), F32),
             pltpu.VMEM((64 * geo.tiles + 64, LANES), F32),
-            pltpu.VMEM((64 * geo.tiles + 64, LANES), F32),
-            pltpu.VMEM((8, 16, pairs * LANES), jnp.int16),
-            pltpu.VMEM((8, 8, LANES), F32),
-            pltpu.VMEM((8, 16, pairs * LANES), jnp.int16),
-            pltpu.VMEM((8, 8, LANES), F32),
+            pltpu.VMEM((8, 16, (SPAN // 2 + 1) * LANES), jnp.int16),
+            pltpu.VMEM((8, 16, (SPAN // 2 + 1) * LANES), jnp.int16),
             pltpu.VMEM((64, LANES), F32),
             pltpu.VMEM((1, geo.channels), I32),
             pltpu.VMEM((16, LANES), I32),
@@ -548,9 +544,9 @@
             dma((2,)),
             dma((4, slots)),
             dma((4, slots)),
-            dma((2, geo.n_sub)),
-            dma((2, geo.n_sub)),
-            dma((2,)),
+            dma((geo.n_sub,)),
+            dma((geo.n_sub,)),
+            dma(()),
         ],
         compiler_params=pltpu.CompilerParams(collective_id=0, has_side_effects=True, vmem_limit_bytes=62 * 2**20),
         name="dedisperse",

time: 43.9 us -> 41.8 us (0.952)
  Pallas kernels: 42.2 us -> 40.2 us
    pallas_call x1, Pallas kernels: 42.2 us -> 40.2 us  [local(): pl.pallas_call(functools.partial(kernel, geo), out_shape=jax.ShapeDtypeSt...]
where the time goes in v3:
time: 41.8 us; the launch traced here: 41.6 us
  Pallas kernels  40.2 us (96%)
  local copies, waits for them, and re-layouts  1.47 us (4%)
    pallas_call x1, Pallas kernels, local(): pl.pallas_call(functools.partial(kernel, geo), out_shape=jax.ShapeDtypeSt...  40.2 us
    unnamed x1, local copies, waits for them, and re-layouts  1.47 us

profile of v3, /device:TPU:1, one launch (start us, length us, event | category | flops | bytes accessed | tf_op | source)
XLA Modules:
  0.0 41.6 jit_solution(17478133794128285314)
XLA Ops:
  0.0 40.2 %dedisperse.1 = f32[128,64]{1,0:T(8,128)} custom-call(bf16[256,4096]{1,0:T(8,128)(2,1)} %spectra_ref.1, s32[1,256]{1,0:T(1,128)} %bitcast.7, s32[16,128]{1,0:T(8,128)} %bitcast.6), custom_call_target="tpu_custom_call" | custom-call | tf_op jit(solution)/shard_map/dedisperse/pallas_call | solution.py:516
  40.2 1.5 %copy.5 = f32[64,8,16]{0,2,1:T(8,128)} copy(f32[64,8,16]{0,2,1:T(8,128)} %bitcast.5) | data formatting | bytes 65536

commit v4 on v3

--- a/solution.py
+++ b/solution.py
@@ -140,9 +140,11 @@
         for k in range(1, self.count):
             source = lax.rem(self.me + k, self.count)
             self.copy(k, source).wait_recv()
+        return jnp.sum(self.slots[...], axis=0)
+
+    def sent(self):
         for k in range(1, self.count):
             self.copy(k, self.me).wait_send()
-        return jnp.sum(self.slots[...], axis=0)
 
 
 def along(values, index, axis):
@@ -449,6 +451,7 @@
         return jnp.where(lane == 8 * g + place, jnp.sum(total, axis=1, keepdims=True), packed)
 
     packed = lax.fori_loop(0, 8, group_power, jnp.zeros((8, LANES), F32), unroll=8)
+    rings = [over_y, over_z]
     over_y = Ring(power_y, y_index, geo.ny, along_y, ring_send.at[2], ring_recv.at[2])
     over_z = Ring(power_z, z_index, geo.nz, along_z, ring_send.at[3], ring_recv.at[3])
     over_y.start(jnp.sum(packed, axis=0, keepdims=True))
@@ -481,12 +484,14 @@
         best[pl.ds(pl.multiple_of(8 * g, 8), 8), :] = kept
         return carry
 
-    lax.fori_loop(0, 4, group_best, 0)
+    lax.fori_loop(0, 4, group_best, 0, unroll=2)
     over_z.start(over_y.total())
-    lax.fori_loop(4, 8, group_best, 0)
+    lax.fori_loop(4, 8, group_best, 0, unroll=2)
     for k in (0, 1, 2, 3, 5, 6, 7):
         swap(k, 4 * (far if k < 4 else near) + lax.rem(place_in_half + k, 4), position).wait_send()
     mean_power = over_z.total() / total_time
+    for ring in rings + [over_y, over_z]:
+        ring.sent()
     inverse = jnp.broadcast_to(1.0 / jnp.sqrt(mean_power + 1e-06), (8, LANES))
     for g in range(8):
         scale = jnp.sum(jnp.where(lane == 8 * g + place, inverse, 0.0), axis=1, keepdims=True)

time: 41.8 us -> 40 us (0.957)
  Pallas kernels: 40.2 us -> 38.4 us
    pallas_call x1, Pallas kernels: 40.2 us -> 38.4 us  [local(): pl.pallas_call(functools.partial(kernel, geo), out_shape=jax.ShapeDtypeSt...]
where the time goes in v4:
time: 40 us; the launch traced here: 39.9 us
  Pallas kernels  38.4 us (96%)
  local copies, waits for them, and re-layouts  1.47 us (4%)
    pallas_call x1, Pallas kernels, local(): pl.pallas_call(functools.partial(kernel, geo), out_shape=jax.ShapeDtypeSt...  38.4 us
    unnamed x1, local copies, waits for them, and re-layouts  1.47 us

profile of v4, /device:TPU:1, one launch (start us, length us, event | category | flops | bytes accessed | tf_op | source)
XLA Modules:
  0.0 39.9 jit_solution(10378630060848500841)
XLA Ops:
  0.0 38.4 %dedisperse.1 = f32[128,64]{1,0:T(8,128)} custom-call(bf16[256,4096]{1,0:T(8,128)(2,1)} %spectra_ref.1, s32[1,256]{1,0:T(1,128)} %bitcast.7, s32[16,128]{1,0:T(8,128)} %bitcast.6), custom_call_target="tpu_custom_call" | custom-call | tf_op jit(solution)/shard_map/dedisperse/pallas_call | solution.py:521
  38.4 1.5 %copy.5 = f32[64,8,16]{0,2,1:T(8,128)} copy(f32[64,8,16]{0,2,1:T(8,128)} %bitcast.5) | data formatting | bytes 65536

commit v5 on v4

--- a/solution.py
+++ b/solution.py
@@ -299,6 +299,8 @@
     @pl.when(jnp.logical_not(not_last))
     def _():
         x[:, pl.ds(right_first, RIGHT * LANES)] = jnp.zeros((geo.channels, RIGHT * LANES), BF16)
+
+    thin[pl.ds(32 * tiles, 64), :] = jnp.zeros((64, LANES), F32)
 
     for copy in small:
         copy.wait()

time: 40 us -> 40 us (level)
  no operation moved by 1% of the time
where the time goes in v5:
time: 40 us; the launch traced here: 39.9 us
  Pallas kernels  38.4 us (96%)
  local copies, waits for them, and re-layouts  1.47 us (4%)
    pallas_call x1, Pallas kernels, local(): pl.pallas_call(functools.partial(kernel, geo), out_shape=jax.ShapeDtypeSt...  38.4 us
    unnamed x1, local copies, waits for them, and re-layouts  1.47 us

profile of v5, /device:TPU:1, one launch (start us, length us, event | category | flops | bytes accessed | tf_op | source)
XLA Modules:
  0.0 39.9 jit_solution(15108350016433357038)
XLA Ops:
  0.0 38.4 %dedisperse.1 = f32[128,64]{1,0:T(8,128)} custom-call(bf16[256,4096]{1,0:T(8,128)(2,1)} %spectra_ref.1, s32[1,256]{1,0:T(1,128)} %bitcast.7, s32[16,128]{1,0:T(8,128)} %bitcast.6), custom_call_target="tpu_custom_call" | custom-call | tf_op jit(solution)/shard_map/dedisperse/pallas_call | solution.py:523
  38.4 1.5 %copy.5 = f32[64,8,16]{0,2,1:T(8,128)} copy(f32[64,8,16]{0,2,1:T(8,128)} %bitcast.5) | data formatting | bytes 65536

commit v6 on v5

--- a/solution.py
+++ b/solution.py
@@ -133,7 +133,7 @@
 
     def start(self, value):
         self.slots[pl.ds(self.me, 1)] = value[None]
-        for k in range(1, self.count):
+        for k in sorted(range(1, self.count), key=lambda k: -min(k, self.count - k)):
             self.copy(k, self.me).start()
 
     def total(self):

time: 40 us -> 40 us (level)
  no operation moved by 1% of the time
where the time goes in v6:
time: 40 us; the launch traced here: 39.9 us
  Pallas kernels  38.4 us (96%)
  local copies, waits for them, and re-layouts  1.47 us (4%)
    pallas_call x1, Pallas kernels, local(): pl.pallas_call(functools.partial(kernel, geo), out_shape=jax.ShapeDtypeSt...  38.4 us
    unnamed x1, local copies, waits for them, and re-layouts  1.47 us

profile of v6, /device:TPU:1, one launch (start us, length us, event | category | flops | bytes accessed | tf_op | source)
XLA Modules:
  0.0 39.9 jit_solution(4580261924669073387)
XLA Ops:
  0.0 38.4 %dedisperse.1 = f32[128,64]{1,0:T(8,128)} custom-call(bf16[256,4096]{1,0:T(8,128)(2,1)} %spectra_ref.1, s32[1,256]{1,0:T(1,128)} %bitcast.7, s32[16,128]{1,0:T(8,128)} %bitcast.6), custom_call_target="tpu_custom_call" | custom-call | tf_op jit(solution)/shard_map/dedisperse/pallas_call | solution.py:523
  38.4 1.5 %copy.5 = f32[64,8,16]{0,2,1:T(8,128)} copy(f32[64,8,16]{0,2,1:T(8,128)} %bitcast.5) | data formatting | bytes 65536
